TPU v7x, 32 devices: a whole 2x2x4 slice. The times are simulated.
32 devices in a mesh: groups: 2 (over x), gx: 16 (over z, y, core).
Axes of the slice: x: 2, y: 2, z: 4, core: 2. Of those that a mesh axis runs over, the one named last changes fastest.
Arguments:
- features: bfloat16 [64, 16, 64, 128], P(('groups', 'gx')), parts along dimension 0, may hold values from -6 to 6
- cotangent: bfloat16 [64, 16, 64, 128], P(('groups', 'gx')), parts along dimension 0, may hold values from -6 to 6
- wall_flags: int32 [64, 16, 128], P(('groups', 'gx')), parts along dimension 0, may hold values 0 or 1
- mode_counts: int32 [64], replicated, may hold values from 1 to 16, as said below
- offsets: int32 [6, 3], replicated, may hold values from -2 to 2, as said below
- point_weight: bfloat16 [64, 64], replicated, may hold values from -0.75 to 0.75
- kernel_weight: bfloat16 [6, 64, 64], replicated, may hold values from -0.3125 to 0.3125
- lap_weight: bfloat16 [64, 64], replicated, may hold values from -0.125 to 0.125
- spec_weight: bfloat16 [16, 64, 64], replicated, may hold values from -1 to 1
- bias: float32 [64], replicated, may hold values from -3 to 3
Outputs:
- input_grad: bfloat16 [64, 16, 64, 128], P(('groups', 'gx')), parts along dimension 0
- kernel_grad: float32 [12, 64, 64], P('groups'), parts along dimension 0
There are 2 independent parts, one for each index of `groups`. A program takes and returns all parts, laid end to end along the dimension named above; an argument that names none is the same for every part. Nothing has to cross between parts.
Inputs may be any that keep to these rules, and one draw needn't show every extreme that they name: Column 0 holds x offsets in -1..1 and both -1 and 1 occur; columns 1 and 2 hold y and z offsets in -2..2, and -2 and 2 occur in each of them. `mode_counts`: some channel keeps 16 modes and some channel keeps 1.
All inputs are finite; a program needn't handle non-finite values. No bound on the sum of `wall_flags` on one device may be relied on, other than what follows from the above.
Results may differ from a plain program's by a relative error of at most 0.0066.
Values may be sent and summed in bfloat16 or wider, within the bound.
A program may use at most 256 MiB of HBM per device.

v0:
```python
from functools import partial
import math
import jax
import jax.numpy as jnp
from jax import lax
from jax.sharding import PartitionSpec as P

RAD = 2


def with_halo(cells, sides, width):
    for axis, dim in sides:
        count = lax.axis_size(axis)
        ends = count - 1
        head = lax.slice_in_dim(cells, 0, width, axis=dim)
        tail = lax.slice_in_dim(cells, cells.shape[dim] - width, cells.shape[dim], axis=dim)
        cells = jnp.concatenate(
            [
                lax.ppermute(tail, axis, [(i, (i + 1) % count) for i in range(ends)]),
                cells,
                lax.ppermute(head, axis, [((i + 1) % count, i) for i in range(ends)]),
            ],
            axis=dim,
        )
    return cells


def basis_table(mode_total, length):
    mode_index = jnp.arange(mode_total, dtype=jnp.float32)[:, None]
    cell_index = jnp.arange(length, dtype=jnp.float32)[None, :]
    phase_angle = math.pi / (2.0 * length) * mode_index * (2.0 * cell_index + 1.0)
    amplitude = jnp.where(mode_index == 0.0, math.sqrt(1.0 / length), math.sqrt(2.0 / length))
    return (amplitude * jnp.cos(phase_angle)).astype(jnp.bfloat16)


def pencil_work(pencil, spec_weight, kept_modes, adjoint):
    basis = basis_table(spec_weight.shape[0], pencil.shape[0])
    coefficients = jnp.einsum(
        "kx,xycz->kycz", basis, pencil, preferred_element_type=jnp.float32
    ).astype(jnp.bfloat16)
    if adjoint:
        masked = coefficients * kept_modes[:, None, :, None].astype(jnp.bfloat16)
        mixed_modes = jnp.einsum(
            "koc,kyoz->kycz", spec_weight, masked, preferred_element_type=jnp.float32
        ).astype(jnp.bfloat16)
    else:
        mixed_modes = jnp.einsum(
            "koc,kycz->kyoz", spec_weight, coefficients, preferred_element_type=jnp.float32
        )
        mixed_modes = (mixed_modes * kept_modes[:, None, :, None]).astype(jnp.bfloat16)
    return jnp.einsum(
        "kx,kyoz->xyoz", basis, mixed_modes, preferred_element_type=jnp.float32
    ).astype(jnp.bfloat16)


def spectral(slab, spec_weight, kept_modes, adjoint):
    result = pencil_work(
        lax.all_to_all(slab, "gx", split_axis=1, concat_axis=0, tiled=True),
        spec_weight,
        kept_modes,
        adjoint,
    )
    return lax.all_to_all(result, "gx", split_axis=0, concat_axis=1, tiled=True)


def laplace_ext(extended):
    padded = jnp.pad(extended, ((0, 0), (1, 1), (0, 0), (1, 1))).astype(jnp.float32)
    centre_cells = padded[1:-1, 1:-1, :, 1:-1]
    neighbours = padded[2:, 1:-1, :, 1:-1] + padded[:-2, 1:-1, :, 1:-1]
    neighbours = neighbours + padded[1:-1, 2:, :, 1:-1] + padded[1:-1, :-2, :, 1:-1]
    neighbours = neighbours + padded[1:-1, 1:-1, :, 2:] + padded[1:-1, 1:-1, :, :-2]
    return (neighbours - 6.0 * centre_cells).astype(jnp.bfloat16)


def pad_sides(extended):
    return jnp.pad(extended, ((0, 0), (RAD, RAD), (0, 0), (RAD, RAD)))


def window_of(padded, offset, direction, slab_shape):
    starts = (
        1 + direction * offset[0],
        RAD + direction * offset[1],
        0,
        RAD + direction * offset[2],
    )
    return lax.dynamic_slice(padded, starts, slab_shape)


def gelu_slope(preact, upstream):
    _, pullback = jax.vjp(partial(jax.nn.gelu, approximate=True), preact)
    return pullback(upstream)[0]


def per_device(
    features,
    cotangent,
    wall_flags,
    mode_counts,
    offsets,
    point_weight,
    kernel_weight,
    lap_weight,
    spec_weight,
    bias,
):
    mode_total = spec_weight.shape[0]
    tile_total = kernel_weight.shape[0]
    kept_modes = (jnp.arange(mode_total, dtype=jnp.int32)[:, None] < mode_counts[None, :]).astype(
        jnp.float32
    )
    fluid_mask = (1 - wall_flags).astype(jnp.float32)[:, :, None, :]
    extended = with_halo(features, (("gx", 0),), 1)
    padded_field = pad_sides(extended)
    local_part = jnp.einsum(
        "oc,xycz->xyoz", point_weight, features, preferred_element_type=jnp.float32
    )
    local_part = local_part + jnp.einsum(
        "oc,xycz->xyoz", lap_weight, laplace_ext(extended), preferred_element_type=jnp.float32
    )
    for tile in range(tile_total):
        moved = window_of(padded_field, offsets[tile], 1, features.shape)
        local_part = local_part + jnp.einsum(
            "oc,xycz->xyoz", kernel_weight[tile], moved, preferred_element_type=jnp.float32
        )
    local_part = local_part + bias[:, None]
    spectral_part = spectral(features, spec_weight, kept_modes, False)
    preact = local_part + spectral_part.astype(jnp.float32)
    weighted = (gelu_slope(preact, cotangent.astype(jnp.float32)) * fluid_mask).astype(jnp.bfloat16)
    spec_grad = spectral(weighted, spec_weight, kept_modes, True)
    ext_grad = with_halo(weighted, (("gx", 0),), 1)
    padded_grad = pad_sides(ext_grad)
    input_grad = jnp.einsum(
        "oc,xyoz->xycz", point_weight, weighted, preferred_element_type=jnp.float32
    )
    input_grad = input_grad + jnp.einsum(
        "oc,xyoz->xycz", lap_weight, laplace_ext(ext_grad), preferred_element_type=jnp.float32
    )
    input_grad = input_grad + spec_grad.astype(jnp.float32)
    tile_grads = []
    for tile in range(tile_total):
        back_moved = window_of(padded_grad, offsets[tile], -1, weighted.shape)
        input_grad = input_grad + jnp.einsum(
            "oc,xyoz->xycz", kernel_weight[tile], back_moved, preferred_element_type=jnp.float32
        )
        tile_grads.append(
            jnp.einsum("xyoz,xycz->oc", back_moved, features, preferred_element_type=jnp.float32)
        )
    local_grad = jnp.stack(tile_grads, axis=0)
    scaling = float(
        lax.axis_size("gx") * features.shape[0] * features.shape[1] * features.shape[3]
    ) ** (-0.5)
    summed = lax.psum(local_grad, "gx")
    return (input_grad.astype(jnp.bfloat16), summed * scaling)


def solution(mesh):
    return jax.shard_map(
        per_device,
        mesh=mesh,
        in_specs=(
            P(("groups", "gx"), None, None, None),
            P(("groups", "gx"), None, None, None),
            P(("groups", "gx"), None, None),
            P(),
            P(),
            P(),
            P(),
            P(),
            P(),
            P(),
        ),
        out_specs=(P(("groups", "gx"), None, None, None), P("groups", None, None)),
        check_vma=False,
    )
```

profile of v0, /device:TPU:0, one launch (start us, length us, event | category | flops | bytes accessed | tf_op | source)
XLA Modules:
  0.0 241.2 jit_solution(13705008029308537028)
XLA Ops:
  8.4 2.4 collective-permute-start
  12.0 1.9 copy.40
  13.9 9.4 %all-to-all-start = ((bf16[2,16,64,128]{3,2,0,1:T(8,128)(2,1)}), bf16[2,16,64,128]{3,2,0,1:T(8,128)(2,1)S(1)}, u32[]{:S(2)}, u32[]{:S(2)}) async-start(bf16[2,16,64,128]{3,2,0,1:T(8,128)(2,1)} %copy.40), calls=%async_computation | async-start | bytes 1048576 | tf_op jit(solution)/shard_map/all_to_all | solution.py:58
  61.1 1.5 fusion.48
  67.4 6.0 %all-to-all-start.1 = ((bf16[32,1,64,128]{3,2,1,0:T(8,128)(2,1)}), bf16[32,1,64,128]{3,2,1,0:T(8,128)(2,1)S(1)}, u32[]{:S(2)}, u32[]{:S(2)}) async-start(bf16[32,1,64,128]{3,2,1,0:T(8,128)(2,1)} %copy.44), calls=%async_computation.1 | async-start | bytes 1048576 | tf_op jit(solution)/shard_map/all_to_all | solution.py:63
  74.2 1.4 fusion.50
  75.7 1.4 fusion.51
  77.1 2.9 %convolution_add_fusion.1 = f32[2,16,128,64]{2,3,1,0:T(8,128)} fusion(f32[2,16,128,64]{2,3,1,0:T(8,128)S(1)} %copy-done.3, f32[4,18,64,130]{3,2,1,0:T(8,128)S(1)} %pad_convert_fusion.1, bf16[64,64]{1,0:T(8,128)(2,1)S(1)} %copy-done.12), kind=kOutput, calls=%fused_computation.37 | convolution fusion | flops 35913728 | bytes 9453568 | tf_op jit(solution)/shard_map/oc,xycz->xyoz/dot_general | solution.py:117
  79.9 8.0 %all-to-all-done.1 = bf16[32,1,64,128]{3,2,1,0:T(8,128)(2,1)S(1)} async-done(((bf16[32,1,64,128]{3,2,1,0:T(8,128)(2,1)}), bf16[32,1,64,128]{3,2,1,0:T(8,128)(2,1)S(1)}, u32[]{:S(2)}, u32[]{:S(2)}) %all-to-all-start.1) | async-done | bytes 524320 | tf_op jit(solution)/shard_map/all_to_all | solution.py:63
  88.7 4.2 %fusion.33 = bf16[2,16,64,128]{3,2,1,0:T(8,128)(2,1)S(1)} fusion(bf16[2,16,64,128]{3,2,1,0:T(8,128)(2,1)} %param.11, f32[2,16,128,64]{2,3,1,0:T(8,128)} %fusion.51, f32[2,16,128,64]{2,3,1,0:T(8,128)} %fusion.50, f32[2,16,128,64]{2,3,1,0:T(8,128)} %fusion.49, f32[2,16,128,64]{2,3,1,0:T(8,128)} %fusion.48, f32[2,16,128,64]{2,3,1,0:T(8,128)S(1)} %fusion.47, ...), kind=kOutput, calls=%fused_computation.72 | convolution fusion | flops 41680896 | bytes 8946188 | tf_op jit(solution)/shard_map/oc,xycz->xyoz/dot_general | solution.py:122
  93.7 1.9 collective-permute-start.2
  97.0 6.9 %all-to-all-start.2 = ((bf16[2,16,64,128]{3,2,0,1:T(8,128)(2,1)}), bf16[2,16,64,128]{3,2,0,1:T(8,128)(2,1)}, u32[]{:S(2)}, u32[]{:S(2)}) async-start(bf16[2,16,64,128]{3,2,0,1:T(8,128)(2,1)} %copy.49), calls=%async_computation.2 | async-start | bytes 1048576 | tf_op jit(solution)/shard_map/all_to_all | solution.py:58
  110.9 1.5 convolution_bitcast_fusion.2
  112.3 1.4 convolution_bitcast_fusion.3
  113.7 4.7 %all-to-all-done.2 = bf16[2,16,64,128]{3,2,0,1:T(8,128)(2,1)} async-done(((bf16[2,16,64,128]{3,2,0,1:T(8,128)(2,1)}), bf16[2,16,64,128]{3,2,0,1:T(8,128)(2,1)}, u32[]{:S(2)}, u32[]{:S(2)}) %all-to-all-start.2) | async-done | bytes 524320 | tf_op jit(solution)/shard_map/all_to_all | solution.py:58
  118.4 1.5 fusion.22
  121.7 4.1 %all-to-all-start.3 = ((bf16[32,1,64,128]{3,2,1,0:T(8,128)(2,1)}), bf16[32,1,64,128]{3,2,1,0:T(8,128)(2,1)S(1)}, u32[]{:S(2)}, u32[]{:S(2)}) async-start(bf16[32,1,64,128]{3,2,1,0:T(8,128)(2,1)} %copy.55), calls=%async_computation.3 | async-start | bytes 1048576 | tf_op jit(solution)/shard_map/all_to_all | solution.py:63
  126.9 1.4 convolution_bitcast_fusion.4
  128.3 1.5 convolution_bitcast_fusion
  129.8 2.9 %pad_convert_fusion = f32[4,18,64,130]{3,2,1,0:T(8,128)} fusion(bf16[4,16,64,128]{3,2,1,0:T(8,128)(2,1)S(1)} %pad_maximum_fusion), kind=kLoop, calls=%fused_computation.12 | loop fusion | flops 599040 | bytes 3444736 | tf_op jit(solution)/shard_map/convert_element_type | solution.py:67
  132.7 89.0 %all-reduce.6.cloned.1.call-done = f32[6,64,64]{2,1,0:T(8,128)} async-done(((f32[6,64,64]{2,1,0:T(8,128)}), f32[6,64,64]{2,1,0:T(8,128)}) %all-reduce.6.cloned.1.call-update) | async-done | bytes 98320 | tf_op jit(solution)/shard_map/psum | solution.py:152
  221.7 1.6 broadcast_multiply_fusion
  223.4 7.5 %fusion.15 = f32[2,16,64,128]{3,2,1,0:T(8,128)S(1)} fusion(f32[2,16,128,64]{2,3,1,0:T(8,128)} %fusion.74, f32[4,18,64,130]{3,2,1,0:T(8,128)} %pad_convert_fusion, bf16[64,64]{1,0:T(8,128)(2,1)S(1)} %copy-done.13, bf16[16,2,1,64,128]{4,3,1,0,2:T(8,128)(2,1)S(1)} %bitcast.306), kind=kOutput, calls=%fused_computation.40 | convolution fusion | flops 36438016 | bytes 9969664 | tf_op jit(solution)/shard_map/oc,xyoz->xycz/dot_general | solution.py:135
  230.8 3.5 %fusion.16 = bf16[2,16,64,128]{3,2,1,0:T(8,128)(2,1)} fusion(f32[2,16,64,128]{3,2,1,0:T(8,128)} %convolution_bitcast_fusion, f32[2,16,64,128]{3,2,1,0:T(8,128)S(1)} %convolution_bitcast_fusion.1, f32[2,16,64,128]{3,2,1,0:T(8,128)} %convolution_bitcast_fusion.2, f32[2,16,64,128]{3,2,1,0:T(8,128)} %convolution_bitcast_fusion.3, ...), kind=kOutput, calls=%fused_computation.43 | convolution fusion | flops 35389440 | bytes 7880716 | tf_op jit(solution)/shard_map/oc,xyoz->xycz/dot_general | solution.py:142
  (70 shorter events, 24.5 us)
Async XLA Ops:
  7.2 57.9 %copy-start = (bf16[16,64,64]{2,1,0:T(8,128)(2,1)S(1)}, bf16[16,64,64]{2,1,0:T(8,128)(2,1)}, u32[]{:S(2)}) copy-start(bf16[16,64,64]{2,1,0:T(8,128)(2,1)} %param.18) | copy-start | bytes 393220
  7.2 16.2 %copy-start.1 = (bf16[2,16,64,128]{3,2,1,0:T(8,128)(2,1)S(1)}, bf16[2,16,64,128]{3,2,1,0:T(8,128)(2,1)}, u32[]{:S(2)}) copy-start(bf16[2,16,64,128]{3,2,1,0:T(8,128)(2,1)} %param.10) | copy-start | bytes 1572868
  7.2 16.2 %copy-start.11 = (s32[64]{0:T(128)S(1)}, s32[64]{0:T(128)}, u32[]{:S(2)}) copy-start(s32[64]{0:T(128)} %param.13) | copy-start | bytes 772
  7.2 16.2 %copy-start.5 = (bf16[64,64]{1,0:T(8,128)(2,1)S(1)}, bf16[64,64]{1,0:T(8,128)(2,1)}, u32[]{:S(2)}) copy-start(bf16[64,64]{1,0:T(8,128)(2,1)} %param.15) | copy-start | bytes 24580
  7.2 17.5 %copy-start.8 = (s32[2,16,128]{2,1,0:T(8,128)S(1)}, s32[2,16,128]{2,1,0:T(8,128)}, u32[]{:S(2)}) copy-start(s32[2,16,128]{2,1,0:T(8,128)} %param.12) | copy-start | bytes 49156
  7.2 17.5 %copy-start.6 = (s32[6,3]{0,1:T(4,128)S(1)}, s32[6,3]{0,1:T(4,128)}, u32[]{:S(2)}) copy-start(s32[6,3]{0,1:T(4,128)} %param.14) | copy-start | bytes 220
  8.4 52.2 %collective-permute-start = (bf16[1,16,64,128]{3,2,1,0:T(8,128)(2,1)S(1)}, bf16[1,16,64,128]{3,2,1,0:T(8,128)(2,1)S(1)}, u32[]{:S(2)}, u32[]{:S(2)}) collective-permute-start(bf16[1,16,64,128]{3,2,1,0:T(8,128)(2,1)S(1)} %get-tuple-element.5), channel_id=1, source_target_pairs={{0,1},{1,2},{2,3},{3,4},{4,5},{5,6},{6,7},{7,8},{8,9},{9,10},{10,1... | collective-permute-start | bytes 786440 | tf_op jit(solution)/shard_map/ppermute | solution.py:19
  10.7 49.9 %collective-permute-start.1 = (bf16[1,16,64,128]{3,2,1,0:T(8,128)(2,1)S(1)}, bf16[1,16,64,128]{3,2,1,0:T(8,128)(2,1)S(1)}, u32[]{:S(2)}, u32[]{:S(2)}) collective-permute-start(bf16[1,16,64,128]{3,2,1,0:T(8,128)(2,1)S(1)} %get-tuple-element.4), channel_id=1, source_target_pairs={{1,0},{2,1},{3,2},{4,3},{5,4},{6,5},{7,6},{8,7},{9,8},{10,9},{11,1... | collective-permute-start | bytes 786440 | tf_op jit(solution)/shard_map/ppermute | solution.py:21
  13.9 46.8 %copy-start.4 = (bf16[6,64,64]{2,1,0:T(8,128)(2,1)S(1)}, bf16[6,64,64]{2,1,0:T(8,128)(2,1)}, u32[]{:S(2)}) copy-start(bf16[6,64,64]{2,1,0:T(8,128)(2,1)} %param.16) | copy-start | bytes 147460
  13.9 50.1 %all-to-all-start = ((bf16[2,16,64,128]{3,2,0,1:T(8,128)(2,1)}), bf16[2,16,64,128]{3,2,0,1:T(8,128)(2,1)S(1)}, u32[]{:S(2)}, u32[]{:S(2)}) async-start(bf16[2,16,64,128]{3,2,0,1:T(8,128)(2,1)} %copy.40), calls=%async_computation | async-start | bytes 1048576 | tf_op jit(solution)/shard_map/all_to_all | solution.py:58
  67.4 20.5 %all-to-all-start.1 = ((bf16[32,1,64,128]{3,2,1,0:T(8,128)(2,1)}), bf16[32,1,64,128]{3,2,1,0:T(8,128)(2,1)S(1)}, u32[]{:S(2)}, u32[]{:S(2)}) async-start(bf16[32,1,64,128]{3,2,1,0:T(8,128)(2,1)} %copy.44), calls=%async_computation.1 | async-start | bytes 1048576 | tf_op jit(solution)/shard_map/all_to_all | solution.py:63
  74.2 2.9 %copy-start.3 = (f32[2,16,128,64]{2,3,1,0:T(8,128)S(1)}, f32[2,16,128,64]{2,3,1,0:T(8,128)}, u32[]{:S(2)}) copy-start(f32[2,16,128,64]{2,3,1,0:T(8,128)} %fusion.76) | copy-start | bytes 3145732
  74.2 2.9 %copy-start.12 = (bf16[64,64]{1,0:T(8,128)(2,1)S(1)}, bf16[64,64]{1,0:T(8,128)(2,1)}, u32[]{:S(2)}) copy-start(bf16[64,64]{1,0:T(8,128)(2,1)} %param.17) | copy-start | bytes 24580
  75.7 13.0 %copy-start.10 = (f32[64]{0:T(128)S(1)}, f32[64]{0:T(128)}, u32[]{:S(2)}) copy-start(f32[64]{0:T(128)} %param.19) | copy-start | bytes 772
  87.9 0.8 copy-start.2
  93.7 11.5 %collective-permute-start.2 = (bf16[1,16,64,128]{3,2,1,0:T(8,128)(2,1)S(1)}, bf16[1,16,64,128]{3,2,1,0:T(8,128)(2,1)S(1)}, u32[]{:S(2)}, u32[]{:S(2)}) collective-permute-start(bf16[1,16,64,128]{3,2,1,0:T(8,128)(2,1)S(1)} %get-tuple-element.2), channel_id=1, source_target_pairs={{0,1},{1,2},{2,3},{3,4},{4,5},{5,6},{6,7},{7,8},{8,9},{9,10},{10,1... | collective-permute-start | bytes 786440 | tf_op jit(solution)/shard_map/ppermute | solution.py:19
  95.7 9.6 %collective-permute-start.3 = (bf16[1,16,64,128]{3,2,1,0:T(8,128)(2,1)S(1)}, bf16[1,16,64,128]{3,2,1,0:T(8,128)(2,1)S(1)}, u32[]{:S(2)}, u32[]{:S(2)}) collective-permute-start(bf16[1,16,64,128]{3,2,1,0:T(8,128)(2,1)S(1)} %get-tuple-element.3), channel_id=1, source_target_pairs={{1,0},{2,1},{3,2},{4,3},{5,4},{6,5},{7,6},{8,7},{9,8},{10,9},{11,1... | collective-permute-start | bytes 786440 | tf_op jit(solution)/shard_map/ppermute | solution.py:21
  97.0 21.5 %all-to-all-start.2 = ((bf16[2,16,64,128]{3,2,0,1:T(8,128)(2,1)}), bf16[2,16,64,128]{3,2,0,1:T(8,128)(2,1)}, u32[]{:S(2)}, u32[]{:S(2)}) async-start(bf16[2,16,64,128]{3,2,0,1:T(8,128)(2,1)} %copy.49), calls=%async_computation.2 | async-start | bytes 1048576 | tf_op jit(solution)/shard_map/all_to_all | solution.py:58
  110.8 7.6 %copy-start.7 = (bf16[16,64]{0,1:T(8,128)(2,1)S(1)}, bf16[16,64]{0,1:T(8,128)(2,1)}, u32[]{:S(2)}) copy-start(bf16[16,64]{0,1:T(8,128)(2,1)} %copy.51) | copy-start | bytes 6148
  110.8 7.6 %copy-start.9 = (f32[32]{0:T(128)S(1)}, f32[32]{0:T(128)}, u32[]{:S(2)}) copy-start(f32[32]{0:T(128)} %multiply_add_fusion) | copy-start | bytes 388
  121.7 101.7 %all-to-all-start.3 = ((bf16[32,1,64,128]{3,2,1,0:T(8,128)(2,1)}), bf16[32,1,64,128]{3,2,1,0:T(8,128)(2,1)S(1)}, u32[]{:S(2)}, u32[]{:S(2)}) async-start(bf16[32,1,64,128]{3,2,1,0:T(8,128)(2,1)} %copy.55), calls=%async_computation.3 | async-start | bytes 1048576 | tf_op jit(solution)/shard_map/all_to_all | solution.py:63
  125.8 95.9 %all-reduce.6.cloned.1.call-start = ((), (), s32[]{:S(2)}) async-start(), calls=%async_computation.4 | async-start | bytes 393216 | tf_op jit(solution)/shard_map/psum | solution.py:152
  129.8 93.6 %copy-start.13 = (bf16[64,64]{1,0:T(8,128)(2,1)S(1)}, bf16[64,64]{1,0:T(8,128)(2,1)}, u32[]{:S(2)}) copy-start(bf16[64,64]{1,0:T(8,128)(2,1)} %param.17) | copy-start | bytes 24580
Sparse Core Ops, SparseCore 0:
  130.6 91.0 all-reduce.5
where the time goes:
time: 242 us; the launch traced here: 241 us
  waiting for transfers between devices  102 us (42%)
  between operations  48.2 us (20%)
  matrix products  43.7 us (18%)
  starting transfers between devices  33.4 us (14%)
  local copies, waits for them, and re-layouts  8.26 us (3%)
  other arithmetic  5.98 us (2%)
    psum x1, waiting for transfers between devices, per_device(): summed = lax.psum(local_grad, 'gx')  89 us
    all_to_all x2, starting transfers between devices, spectral(): lax.all_to_all(slab, 'gx', split_axis=1, concat_axis=0, tiled=True)  16.4 us
    dot_general x6, matrix products, per_device(): jnp.einsum('oc,xycz->xyoz', kernel_weight[tile], moved, preferred_element...  10.4 us
    all_to_all x2, starting transfers between devices, spectral(): return lax.all_to_all(result, 'gx', split_axis=0, concat_axis=1, tiled=True)  10.1 us
    dot_general x6, matrix products, per_device(): jnp.einsum('oc,xyoz->xycz', kernel_weight[tile], back_moved, preferred_el...  9.73 us
    all_to_all x2, waiting for transfers between devices, spectral(): return lax.all_to_all(result, 'gx', split_axis=0, concat_axis=1, tiled=True)  7.95 us
    dot_general x1, matrix products, per_device(): jnp.einsum('oc,xyoz->xycz', lap_weight, laplace_ext(ext_grad), preferred_...  7.47 us
    dot_general x6, matrix products, per_device(): jnp.einsum('xyoz,xycz->oc', back_moved, features, preferred_element_type=...  6.05 us
  transfers between devices with their start and end apart: 9, of which 3 were waited for; matrix products, arithmetic and copies ran while one was open for 14% of the time, Pallas kernels for 0%

commit v1 on v0

--- a/solution.py
+++ b/solution.py
@@ -6,6 +6,29 @@
 from jax.sharding import PartitionSpec as P
 
 RAD = 2
+
+
+def cut_along(value, dim, size):
+    lengths = value.shape
+    tiles = value.reshape(*lengths[:dim], size, lengths[dim] // size, *lengths[dim + 1 :])
+    return jnp.moveaxis(tiles, dim, 0)
+
+
+def in_order(pieces, dim):
+    pieces = jnp.moveaxis(pieces, 0, dim)
+    dims = pieces.shape
+    return pieces.reshape(*dims[:dim], dims[dim] * dims[dim + 1], *dims[dim + 2 :])
+
+
+def exchange_in_pairs(value, axis, split_dim, concat_dim):
+    size, index = (lax.axis_size(axis), lax.axis_index(axis))
+    parts = cut_along(value, split_dim, size)
+    outs = [parts[index]]
+    for turn in range(1, size):
+        sent = parts[index ^ turn]
+        outs.append(lax.ppermute(sent, axis, [(i, i ^ turn) for i in range(size)]))
+    parts = jnp.stack(outs)[index ^ jnp.arange(size)]
+    return in_order(parts, concat_dim)
 
 
 def with_halo(cells, sides, width):
@@ -54,12 +77,7 @@
 
 
 def spectral(slab, spec_weight, kept_modes, adjoint):
-    result = pencil_work(
-        lax.all_to_all(slab, "gx", split_axis=1, concat_axis=0, tiled=True),
-        spec_weight,
-        kept_modes,
-        adjoint,
-    )
+    result = pencil_work(exchange_in_pairs(slab, "gx", 1, 0), spec_weight, kept_modes, adjoint)
     return lax.all_to_all(result, "gx", split_axis=0, concat_axis=1, tiled=True)
 
 

time: 242 us -> 270 us (1.12)
  starting transfers between devices: 33.4 us -> 61.3 us
  matrix products: 43.7 us -> 38.9 us
    ppermute x0 -> x30, starting transfers between devices: none -> 43 us  [exchange_in_pairs(): outs.append(lax.ppermute(sent, axis, [(i, i ^ turn) for i in range(size)]))]
    all_to_all x2 -> x0, starting transfers between devices: 16.4 us -> none  [spectral(): lax.all_to_all(slab, 'gx', split_axis=1, concat_axis=0, tiled=True)]
    ppermute x0 -> x30, waiting for transfers between devices: none -> 13.3 us  [exchange_in_pairs(): outs.append(lax.ppermute(sent, axis, [(i, i ^ turn) for i in range(size)]))]
    all_to_all x2 -> x0, waiting for transfers between devices: 4.71 us -> none  [spectral(): lax.all_to_all(slab, 'gx', split_axis=1, concat_axis=0, tiled=True)]
    psum x1, waiting for transfers between devices: 89 us -> 85.2 us  [per_device(): summed = lax.psum(local_grad, 'gx')]
    dot_general x6, matrix products: 6.05 us -> 2.34 us  [per_device(): jnp.einsum('xyoz,xycz->oc', back_moved, features, preferred_element_type=...]
    all_to_all x2, waiting for transfers between devices: 7.95 us -> 4.45 us  [spectral(): return lax.all_to_all(result, 'gx', split_axis=0, concat_axis=1, tiled=True)]
  transfers between devices with their start and end apart: 9 -> 37, of which waited for: 3 -> 10; matrix products, arithmetic and copies ran while one was open for 14% -> 13% of each run, Pallas kernels for 0% -> 0%
where the time goes in v1:
time: 270 us; the launch traced here: 269 us
  waiting for transfers between devices  103 us (38%)
  starting transfers between devices  61.3 us (23%)
  between operations  48.7 us (18%)
  matrix products  38.9 us (14%)
  local copies, waits for them, and re-layouts  10.6 us (4%)
  other arithmetic  6.13 us (2%)
    psum x1, waiting for transfers between devices, per_device(): summed = lax.psum(local_grad, 'gx')  85.2 us
    ppermute x30, starting transfers between devices, exchange_in_pairs(): outs.append(lax.ppermute(sent, axis, [(i, i ^ turn) for i in range(size)]))  43 us
    ppermute x30, waiting for transfers between devices, exchange_in_pairs(): outs.append(lax.ppermute(sent, axis, [(i, i ^ turn) for i in range(size)]))  13.3 us
    all_to_all x2, starting transfers between devices, spectral(): return lax.all_to_all(result, 'gx', split_axis=0, concat_axis=1, tiled=True)  10.8 us
    dot_general x6, matrix products, per_device(): jnp.einsum('oc,xycz->xyoz', kernel_weight[tile], moved, preferred_element...  10.4 us
    dot_general x6, matrix products, per_device(): jnp.einsum('oc,xyoz->xycz', kernel_weight[tile], back_moved, preferred_el...  9.76 us
    dot_general x1, matrix products, per_device(): jnp.einsum('oc,xyoz->xycz', lap_weight, laplace_ext(ext_grad), preferred_...  7.87 us
  transfers between devices with their start and end apart: 37, of which 10 were waited for; matrix products, arithmetic and copies ran while one was open for 13% of the time, Pallas kernels for 0%

profile of v1, /device:TPU:0, one launch (start us, length us, event | category | flops | bytes accessed | tf_op | source)
XLA Modules:
  0.0 268.6 jit_solution(2034876682013506445)
XLA Ops:
  9.0 2.6 collective-permute-start.3
  16.0 2.0 fusion.150
  54.2 2.7 %collective-permute-start.7 = (bf16[2,1,64,128]{3,2,0,1:T(8,128)(2,1)S(1)}, bf16[2,1,64,128]{3,2,0,1:T(8,128)(2,1)S(1)}, u32[]{:S(2)}, u32[]{:S(2)}) collective-permute-start(bf16[2,1,64,128]{3,2,0,1:T(8,128)(2,1)S(1)} %get-tuple-element.29), channel_id=1, source_target_pairs={{0,6},{1,7},{2,4},{3,5},{4,2},{5,3},{6,0},{7,1},{8,14},{9,15},{10,... | collective-permute-start | bytes 98312 | tf_op jit(solution)/shard_map/ppermute | solution.py:29
  57.1 2.8 %collective-permute-start.9 = (bf16[2,1,64,128]{3,2,0,1:T(8,128)(2,1)S(1)}, bf16[2,1,64,128]{3,2,0,1:T(8,128)(2,1)S(1)}, u32[]{:S(2)}, u32[]{:S(2)}) collective-permute-start(bf16[2,1,64,128]{3,2,0,1:T(8,128)(2,1)S(1)} %get-tuple-element.27), channel_id=1, source_target_pairs={{0,8},{1,9},{2,10},{3,11},{4,12},{5,13},{6,14},{7,15},{8,0},{9,1},... | collective-permute-start | bytes 98312 | tf_op jit(solution)/shard_map/ppermute | solution.py:29
  60.0 3.6 %collective-permute-start.11 = (bf16[2,1,64,128]{3,2,0,1:T(8,128)(2,1)S(1)}, bf16[2,1,64,128]{3,2,0,1:T(8,128)(2,1)S(1)}, u32[]{:S(2)}, u32[]{:S(2)}) collective-permute-start(bf16[2,1,64,128]{3,2,0,1:T(8,128)(2,1)S(1)} %get-tuple-element.25), channel_id=1, source_target_pairs={{0,10},{1,11},{2,8},{3,9},{4,14},{5,15},{6,12},{7,13},{8,2},{9,3},... | collective-permute-start | bytes 98312 | tf_op jit(solution)/shard_map/ppermute | solution.py:29
  63.7 3.6 %collective-permute-start.13 = (bf16[2,1,64,128]{3,2,0,1:T(8,128)(2,1)S(1)}, bf16[2,1,64,128]{3,2,0,1:T(8,128)(2,1)S(1)}, u32[]{:S(2)}, u32[]{:S(2)}) collective-permute-start(bf16[2,1,64,128]{3,2,0,1:T(8,128)(2,1)S(1)} %get-tuple-element.23), channel_id=1, source_target_pairs={{0,12},{1,13},{2,14},{3,15},{4,8},{5,9},{6,10},{7,11},{8,4},{9,5},... | collective-permute-start | bytes 98312 | tf_op jit(solution)/shard_map/ppermute | solution.py:29
  67.5 4.5 %collective-permute-start.15 = (bf16[2,1,64,128]{3,2,0,1:T(8,128)(2,1)S(1)}, bf16[2,1,64,128]{3,2,0,1:T(8,128)(2,1)S(1)}, u32[]{:S(2)}, u32[]{:S(2)}) collective-permute-start(bf16[2,1,64,128]{3,2,0,1:T(8,128)(2,1)S(1)} %get-tuple-element.35), channel_id=1, source_target_pairs={{0,14},{1,15},{2,12},{3,13},{4,10},{5,11},{6,8},{7,9},{8,6},{9,7},... | collective-permute-start | bytes 98312 | tf_op jit(solution)/shard_map/ppermute | solution.py:29
  72.1 2.2 collective-permute-start
  75.8 2.3 collective-permute-done.16
  80.9 5.6 %all-to-all-start = ((bf16[32,1,64,128]{3,2,1,0:T(8,128)(2,1)}), bf16[32,1,64,128]{3,2,1,0:T(8,128)(2,1)S(1)}, u32[]{:S(2)}, u32[]{:S(2)}) async-start(bf16[32,1,64,128]{3,2,1,0:T(8,128)(2,1)} %copy.111), calls=%async_computation | async-start | bytes 1048576 | tf_op jit(solution)/shard_map/all_to_all | solution.py:81
  93.6 2.9 %convolution_add_fusion.1 = f32[2,16,128,64]{2,3,1,0:T(8,128)} fusion(f32[2,16,128,64]{2,3,1,0:T(8,128)S(1)} %copy-done.3, f32[4,18,64,130]{3,2,1,0:T(8,128)S(1)} %pad_convert_fusion.1, bf16[64,64]{1,0:T(8,128)(2,1)S(1)} %copy-done.8), kind=kOutput, calls=%fused_computation.39 | convolution fusion | flops 35913728 | bytes 9453568 | tf_op jit(solution)/shard_map/oc,xycz->xyoz/dot_general | solution.py:135
  96.5 4.4 %all-to-all-done = bf16[32,1,64,128]{3,2,1,0:T(8,128)(2,1)S(1)} async-done(((bf16[32,1,64,128]{3,2,1,0:T(8,128)(2,1)}), bf16[32,1,64,128]{3,2,1,0:T(8,128)(2,1)S(1)}, u32[]{:S(2)}, u32[]{:S(2)}) %all-to-all-start) | async-done | bytes 524320 | tf_op jit(solution)/shard_map/all_to_all | solution.py:81
  101.7 4.2 %fusion.33 = bf16[2,16,64,128]{3,2,1,0:T(8,128)(2,1)S(1)} fusion(bf16[2,16,64,128]{3,2,1,0:T(8,128)(2,1)} %param.11, f32[2,16,128,64]{2,3,1,0:T(8,128)} %fusion.51, f32[2,16,128,64]{2,3,1,0:T(8,128)} %fusion.50, f32[2,16,128,64]{2,3,1,0:T(8,128)} %fusion.49, f32[2,16,128,64]{2,3,1,0:T(8,128)} %fusion.48, f32[2,16,128,64]{2,3,1,0:T(8,128)S(1)} %fusion.47, ...), kind=kOutput, calls=%fused_computation.74 | convolution fusion | flops 41680896 | bytes 8945932 | tf_op jit(solution)/shard_map/oc,xycz->xyoz/dot_general | solution.py:140
  107.5 2.4 collective-permute-start.17
  111.4 3.1 %collective-permute-start.20 = (bf16[2,1,64,128]{3,2,0,1:T(8,128)(2,1)S(1)}, bf16[2,1,64,128]{3,2,0,1:T(8,128)(2,1)S(1)}, u32[]{:S(2)}, u32[]{:S(2)}) collective-permute-start(bf16[2,1,64,128]{3,2,0,1:T(8,128)(2,1)S(1)} %get-tuple-element.14), channel_id=1, source_target_pairs={{0,2},{1,3},{2,0},{3,1},{4,6},{5,7},{6,4},{7,5},{8,10},{9,11},{10,... | collective-permute-start | bytes 98312 | tf_op jit(solution)/shard_map/ppermute | solution.py:29
  116.2 3.5 %collective-permute-done.20 = bf16[2,1,64,128]{3,2,0,1:T(8,128)(2,1)S(1)} collective-permute-done((bf16[2,1,64,128]{3,2,0,1:T(8,128)(2,1)S(1)}, bf16[2,1,64,128]{3,2,0,1:T(8,128)(2,1)S(1)}, u32[]{:S(2)}, u32[]{:S(2)}) %collective-permute-start.20) | collective-permute-done | bytes 32800 | tf_op jit(solution)/shard_map/ppermute | solution.py:29
  119.7 3.2 %collective-permute-start.24 = (bf16[2,1,64,128]{3,2,0,1:T(8,128)(2,1)S(1)}, bf16[2,1,64,128]{3,2,0,1:T(8,128)(2,1)S(1)}, u32[]{:S(2)}, u32[]{:S(2)}) collective-permute-start(bf16[2,1,64,128]{3,2,0,1:T(8,128)(2,1)S(1)} %get-tuple-element.10), channel_id=1, source_target_pairs={{0,6},{1,7},{2,4},{3,5},{4,2},{5,3},{6,0},{7,1},{8,14},{9,15},{10,... | collective-permute-start | bytes 98312 | tf_op jit(solution)/shard_map/ppermute | solution.py:29
  136.7 3.0 %collective-permute-start.33 = (bf16[2,1,64,128]{3,2,1,0:T(8,128)(2,1)S(1)}, bf16[2,1,64,128]{3,2,1,0:T(8,128)(2,1)S(1)}, u32[]{:S(2)}, u32[]{:S(2)}) collective-permute-start(bf16[2,1,64,128]{3,2,1,0:T(8,128)(2,1)S(1)} %get-tuple-element.2), channel_id=1, source_target_pairs={{0,15},{1,14},{2,13},{3,12},{4,11},{5,10},{6,9},{7,8},{8,7},{9,6},... | collective-permute-start | bytes 98312 | tf_op jit(solution)/shard_map/ppermute | solution.py:29
  139.7 2.6 collective-permute-done.32
  145.7 5.2 %all-to-all-start.1 = ((bf16[32,1,64,128]{3,2,1,0:T(8,128)(2,1)}), bf16[32,1,64,128]{3,2,1,0:T(8,128)(2,1)}, u32[]{:S(2)}, u32[]{:S(2)}) async-start(bf16[32,1,64,128]{3,2,1,0:T(8,128)(2,1)} %copy.135), calls=%async_computation.1 | async-start | bytes 1048576 | tf_op jit(solution)/shard_map/all_to_all | solution.py:81
  160.5 2.9 %pad_convert_fusion = f32[4,18,64,130]{3,2,1,0:T(8,128)} fusion(bf16[4,16,64,128]{3,2,1,0:T(8,128)(2,1)S(1)} %pad_maximum_fusion), kind=kLoop, calls=%fused_computation.14 | loop fusion | flops 599040 | bytes 3444736 | tf_op jit(solution)/shard_map/convert_element_type | solution.py:85
  163.4 85.2 %all-reduce.6.cloned.1.call-done = f32[6,64,64]{2,1,0:T(8,128)} async-done(((f32[6,64,64]{2,1,0:T(8,128)}), f32[6,64,64]{2,1,0:T(8,128)}) %all-reduce.6.cloned.1.call-update) | async-done | bytes 98320 | tf_op jit(solution)/shard_map/psum | solution.py:170
  250.3 7.9 %fusion.15 = f32[2,16,64,128]{3,2,1,0:T(8,128)S(1)} fusion(f32[2,16,128,64]{2,3,1,0:T(8,128)} %fusion.74, f32[4,18,64,130]{3,2,1,0:T(8,128)} %pad_convert_fusion, bf16[64,64]{1,0:T(8,128)(2,1)S(1)} %copy-done.9, bf16[16,2,1,64,128]{4,3,1,0,2:T(8,128)(2,1)} %bitcast.201), kind=kOutput, calls=%fused_computation.42 | convolution fusion | flops 36438016 | bytes 9969664 | tf_op jit(solution)/shard_map/oc,xyoz->xycz/dot_general | solution.py:153
  258.2 3.5 %fusion.16 = bf16[2,16,64,128]{3,2,1,0:T(8,128)(2,1)} fusion(f32[2,16,64,128]{3,2,1,0:T(8,128)} %convolution_bitcast_fusion, f32[2,16,64,128]{3,2,1,0:T(8,128)} %convolution_bitcast_fusion.1, f32[2,16,64,128]{3,2,1,0:T(8,128)} %convolution_bitcast_fusion.2, f32[2,16,64,128]{3,2,1,0:T(8,128)S(1)} %convolution_bitcast_fusion.3, ...), kind=kOutput, calls=%fused_computation.45 | convolution fusion | flops 35389440 | bytes 7880716 | tf_op jit(solution)/shard_map/oc,xyoz->xycz/dot_general | solution.py:160
  (154 shorter events, 54.0 us)
Async XLA Ops:
  8.5 45.7 %collective-permute-start.2 = (bf16[2,1,64,128]{3,2,0,1:T(8,128)(2,1)S(1)}, bf16[2,1,64,128]{3,2,0,1:T(8,128)(2,1)S(1)}, u32[]{:S(2)}, u32[]{:S(2)}) collective-permute-start(bf16[2,1,64,128]{3,2,0,1:T(8,128)(2,1)S(1)} %get-tuple-element.34), channel_id=1, source_target_pairs={{0,1},{1,0},{2,3},{3,2},{4,5},{5,4},{6,7},{7,6},{8,9},{9,8},{10,11... | collective-permute-start | bytes 98312 | tf_op jit(solution)/shard_map/ppermute | solution.py:29
  9.0 47.9 %collective-permute-start.3 = (bf16[2,1,64,128]{3,2,0,1:T(8,128)(2,1)S(1)}, bf16[2,1,64,128]{3,2,0,1:T(8,128)(2,1)S(1)}, u32[]{:S(2)}, u32[]{:S(2)}) collective-permute-start(bf16[2,1,64,128]{3,2,0,1:T(8,128)(2,1)S(1)} %get-tuple-element.33), channel_id=1, source_target_pairs={{0,2},{1,3},{2,0},{3,1},{4,6},{5,7},{6,4},{7,5},{8,10},{9,11},{10,... | collective-permute-start | bytes 98312 | tf_op jit(solution)/shard_map/ppermute | solution.py:29
  11.6 45.5 %collective-permute-start.4 = (bf16[2,1,64,128]{3,2,0,1:T(8,128)(2,1)S(1)}, bf16[2,1,64,128]{3,2,0,1:T(8,128)(2,1)S(1)}, u32[]{:S(2)}, u32[]{:S(2)}) collective-permute-start(bf16[2,1,64,128]{3,2,0,1:T(8,128)(2,1)S(1)} %get-tuple-element.32), channel_id=1, source_target_pairs={{0,3},{1,2},{2,1},{3,0},{4,7},{5,6},{6,5},{7,4},{8,11},{9,10},{10,... | collective-permute-start | bytes 98312 | tf_op jit(solution)/shard_map/ppermute | solution.py:29
  11.7 48.2 %collective-permute-start.5 = (bf16[2,1,64,128]{3,2,0,1:T(8,128)(2,1)S(1)}, bf16[2,1,64,128]{3,2,0,1:T(8,128)(2,1)S(1)}, u32[]{:S(2)}, u32[]{:S(2)}) collective-permute-start(bf16[2,1,64,128]{3,2,0,1:T(8,128)(2,1)S(1)} %get-tuple-element.31), channel_id=1, source_target_pairs={{0,4},{1,5},{2,6},{3,7},{4,0},{5,1},{6,2},{7,3},{8,12},{9,13},{10,... | collective-permute-start | bytes 98312 | tf_op jit(solution)/shard_map/ppermute | solution.py:29
  13.5 46.5 %collective-permute-start.6 = (bf16[2,1,64,128]{3,2,0,1:T(8,128)(2,1)S(1)}, bf16[2,1,64,128]{3,2,0,1:T(8,128)(2,1)S(1)}, u32[]{:S(2)}, u32[]{:S(2)}) collective-permute-start(bf16[2,1,64,128]{3,2,0,1:T(8,128)(2,1)S(1)} %get-tuple-element.30), channel_id=1, source_target_pairs={{0,5},{1,4},{2,7},{3,6},{4,1},{5,0},{6,3},{7,2},{8,13},{9,12},{10,... | collective-permute-start | bytes 98312 | tf_op jit(solution)/shard_map/ppermute | solution.py:29
  54.2 9.3 %collective-permute-start.7 = (bf16[2,1,64,128]{3,2,0,1:T(8,128)(2,1)S(1)}, bf16[2,1,64,128]{3,2,0,1:T(8,128)(2,1)S(1)}, u32[]{:S(2)}, u32[]{:S(2)}) collective-permute-start(bf16[2,1,64,128]{3,2,0,1:T(8,128)(2,1)S(1)} %get-tuple-element.29), channel_id=1, source_target_pairs={{0,6},{1,7},{2,4},{3,5},{4,2},{5,3},{6,0},{7,1},{8,14},{9,15},{10,... | collective-permute-start | bytes 98312 | tf_op jit(solution)/shard_map/ppermute | solution.py:29
  56.9 6.8 %collective-permute-start.8 = (bf16[2,1,64,128]{3,2,0,1:T(8,128)(2,1)S(1)}, bf16[2,1,64,128]{3,2,0,1:T(8,128)(2,1)S(1)}, u32[]{:S(2)}, u32[]{:S(2)}) collective-permute-start(bf16[2,1,64,128]{3,2,0,1:T(8,128)(2,1)S(1)} %get-tuple-element.28), channel_id=1, source_target_pairs={{0,7},{1,6},{2,5},{3,4},{4,3},{5,2},{6,1},{7,0},{8,15},{9,14},{10,... | collective-permute-start | bytes 98312 | tf_op jit(solution)/shard_map/ppermute | solution.py:29
  57.1 10.3 %collective-permute-start.9 = (bf16[2,1,64,128]{3,2,0,1:T(8,128)(2,1)S(1)}, bf16[2,1,64,128]{3,2,0,1:T(8,128)(2,1)S(1)}, u32[]{:S(2)}, u32[]{:S(2)}) collective-permute-start(bf16[2,1,64,128]{3,2,0,1:T(8,128)(2,1)S(1)} %get-tuple-element.27), channel_id=1, source_target_pairs={{0,8},{1,9},{2,10},{3,11},{4,12},{5,13},{6,14},{7,15},{8,0},{9,1},... | collective-permute-start | bytes 98312 | tf_op jit(solution)/shard_map/ppermute | solution.py:29
  59.9 7.6 %collective-permute-start.10 = (bf16[2,1,64,128]{3,2,0,1:T(8,128)(2,1)S(1)}, bf16[2,1,64,128]{3,2,0,1:T(8,128)(2,1)S(1)}, u32[]{:S(2)}, u32[]{:S(2)}) collective-permute-start(bf16[2,1,64,128]{3,2,0,1:T(8,128)(2,1)S(1)} %get-tuple-element.26), channel_id=1, source_target_pairs={{0,9},{1,8},{2,11},{3,10},{4,13},{5,12},{6,15},{7,14},{8,1},{9,0},... | collective-permute-start | bytes 98312 | tf_op jit(solution)/shard_map/ppermute | solution.py:29
  60.0 12.0 %collective-permute-start.11 = (bf16[2,1,64,128]{3,2,0,1:T(8,128)(2,1)S(1)}, bf16[2,1,64,128]{3,2,0,1:T(8,128)(2,1)S(1)}, u32[]{:S(2)}, u32[]{:S(2)}) collective-permute-start(bf16[2,1,64,128]{3,2,0,1:T(8,128)(2,1)S(1)} %get-tuple-element.25), channel_id=1, source_target_pairs={{0,10},{1,11},{2,8},{3,9},{4,14},{5,15},{6,12},{7,13},{8,2},{9,3},... | collective-permute-start | bytes 98312 | tf_op jit(solution)/shard_map/ppermute | solution.py:29
  63.6 8.6 %collective-permute-start.12 = (bf16[2,1,64,128]{3,2,0,1:T(8,128)(2,1)S(1)}, bf16[2,1,64,128]{3,2,0,1:T(8,128)(2,1)S(1)}, u32[]{:S(2)}, u32[]{:S(2)}) collective-permute-start(bf16[2,1,64,128]{3,2,0,1:T(8,128)(2,1)S(1)} %get-tuple-element.24), channel_id=1, source_target_pairs={{0,11},{1,10},{2,9},{3,8},{4,15},{5,14},{6,13},{7,12},{8,3},{9,2},... | collective-permute-start | bytes 98312 | tf_op jit(solution)/shard_map/ppermute | solution.py:29
  63.7 10.7 %collective-permute-start.13 = (bf16[2,1,64,128]{3,2,0,1:T(8,128)(2,1)S(1)}, bf16[2,1,64,128]{3,2,0,1:T(8,128)(2,1)S(1)}, u32[]{:S(2)}, u32[]{:S(2)}) collective-permute-start(bf16[2,1,64,128]{3,2,0,1:T(8,128)(2,1)S(1)} %get-tuple-element.23), channel_id=1, source_target_pairs={{0,12},{1,13},{2,14},{3,15},{4,8},{5,9},{6,10},{7,11},{8,4},{9,5},... | collective-permute-start | bytes 98312 | tf_op jit(solution)/shard_map/ppermute | solution.py:29
  67.4 8.4 %collective-permute-start.14 = (bf16[2,1,64,128]{3,2,0,1:T(8,128)(2,1)S(1)}, bf16[2,1,64,128]{3,2,0,1:T(8,128)(2,1)S(1)}, u32[]{:S(2)}, u32[]{:S(2)}) collective-permute-start(bf16[2,1,64,128]{3,2,0,1:T(8,128)(2,1)S(1)} %get-tuple-element.22), channel_id=1, source_target_pairs={{0,13},{1,12},{2,15},{3,14},{4,9},{5,8},{6,11},{7,10},{8,5},{9,4},... | collective-permute-start | bytes 98312 | tf_op jit(solution)/shard_map/ppermute | solution.py:29
  67.5 8.3 %collective-permute-start.15 = (bf16[2,1,64,128]{3,2,0,1:T(8,128)(2,1)S(1)}, bf16[2,1,64,128]{3,2,0,1:T(8,128)(2,1)S(1)}, u32[]{:S(2)}, u32[]{:S(2)}) collective-permute-start(bf16[2,1,64,128]{3,2,0,1:T(8,128)(2,1)S(1)} %get-tuple-element.35), channel_id=1, source_target_pairs={{0,14},{1,15},{2,12},{3,13},{4,10},{5,11},{6,8},{7,9},{8,6},{9,7},... | collective-permute-start | bytes 98312 | tf_op jit(solution)/shard_map/ppermute | solution.py:29
  72.1 14.3 %collective-permute-start = (bf16[1,16,64,128]{3,2,1,0:T(8,128)(2,1)S(1)}, bf16[1,16,64,128]{3,2,1,0:T(8,128)(2,1)S(1)}, u32[]{:S(2)}, u32[]{:S(2)}) collective-permute-start(bf16[1,16,64,128]{3,2,1,0:T(8,128)(2,1)S(1)} %get-tuple-element.20), channel_id=1, source_target_pairs={{0,1},{1,2},{2,3},{3,4},{4,5},{5,6},{6,7},{7,8},{8,9},{9,10},{10,1... | collective-permute-start | bytes 786440 | tf_op jit(solution)/shard_map/ppermute | solution.py:42
  74.4 12.2 %collective-permute-start.1 = (bf16[1,16,64,128]{3,2,1,0:T(8,128)(2,1)S(1)}, bf16[1,16,64,128]{3,2,1,0:T(8,128)(2,1)S(1)}, u32[]{:S(2)}, u32[]{:S(2)}) collective-permute-start(bf16[1,16,64,128]{3,2,1,0:T(8,128)(2,1)S(1)} %get-tuple-element.19), channel_id=1, source_target_pairs={{1,0},{2,1},{3,2},{4,3},{5,4},{6,5},{7,6},{8,7},{9,8},{10,9},{11,1... | collective-permute-start | bytes 786440 | tf_op jit(solution)/shard_map/ppermute | solution.py:44
  80.9 20.0 %all-to-all-start = ((bf16[32,1,64,128]{3,2,1,0:T(8,128)(2,1)}), bf16[32,1,64,128]{3,2,1,0:T(8,128)(2,1)S(1)}, u32[]{:S(2)}, u32[]{:S(2)}) async-start(bf16[32,1,64,128]{3,2,1,0:T(8,128)(2,1)} %copy.111), calls=%async_computation | async-start | bytes 1048576 | tf_op jit(solution)/shard_map/all_to_all | solution.py:81
  107.5 7.1 %collective-permute-start.19 = (bf16[2,1,64,128]{3,2,0,1:T(8,128)(2,1)S(1)}, bf16[2,1,64,128]{3,2,0,1:T(8,128)(2,1)S(1)}, u32[]{:S(2)}, u32[]{:S(2)}) collective-permute-start(bf16[2,1,64,128]{3,2,0,1:T(8,128)(2,1)S(1)} %get-tuple-element.15), channel_id=1, source_target_pairs={{0,1},{1,0},{2,3},{3,2},{4,5},{5,4},{6,7},{7,6},{8,9},{9,8},{10,11... | collective-permute-start | bytes 98312 | tf_op jit(solution)/shard_map/ppermute | solution.py:29
  107.5 43.5 %collective-permute-start.17 = (bf16[1,16,64,128]{3,2,1,0:T(8,128)(2,1)S(1)}, bf16[1,16,64,128]{3,2,1,0:T(8,128)(2,1)S(1)}, u32[]{:S(2)}, u32[]{:S(2)}) collective-permute-start(bf16[1,16,64,128]{3,2,1,0:T(8,128)(2,1)S(1)} %get-tuple-element.17), channel_id=1, source_target_pairs={{0,1},{1,2},{2,3},{3,4},{4,5},{5,6},{6,7},{7,8},{8,9},{9,10},{10,1... | collective-permute-start | bytes 786440 | tf_op jit(solution)/shard_map/ppermute | solution.py:42
  110.0 41.1 %collective-permute-start.18 = (bf16[1,16,64,128]{3,2,1,0:T(8,128)(2,1)S(1)}, bf16[1,16,64,128]{3,2,1,0:T(8,128)(2,1)S(1)}, u32[]{:S(2)}, u32[]{:S(2)}) collective-permute-start(bf16[1,16,64,128]{3,2,1,0:T(8,128)(2,1)S(1)} %get-tuple-element.18), channel_id=1, source_target_pairs={{1,0},{2,1},{3,2},{4,3},{5,4},{6,5},{7,6},{8,7},{9,8},{10,9},{11,1... | collective-permute-start | bytes 786440 | tf_op jit(solution)/shard_map/ppermute | solution.py:44
  111.4 8.2 %collective-permute-start.20 = (bf16[2,1,64,128]{3,2,0,1:T(8,128)(2,1)S(1)}, bf16[2,1,64,128]{3,2,0,1:T(8,128)(2,1)S(1)}, u32[]{:S(2)}, u32[]{:S(2)}) collective-permute-start(bf16[2,1,64,128]{3,2,0,1:T(8,128)(2,1)S(1)} %get-tuple-element.14), channel_id=1, source_target_pairs={{0,2},{1,3},{2,0},{3,1},{4,6},{5,7},{6,4},{7,5},{8,10},{9,11},{10,... | collective-permute-start | bytes 98312 | tf_op jit(solution)/shard_map/ppermute | solution.py:29
  114.6 8.2 %collective-permute-start.22 = (bf16[2,1,64,128]{3,2,0,1:T(8,128)(2,1)S(1)}, bf16[2,1,64,128]{3,2,0,1:T(8,128)(2,1)S(1)}, u32[]{:S(2)}, u32[]{:S(2)}) collective-permute-start(bf16[2,1,64,128]{3,2,0,1:T(8,128)(2,1)S(1)} %get-tuple-element.12), channel_id=1, source_target_pairs={{0,4},{1,5},{2,6},{3,7},{4,0},{5,1},{6,2},{7,3},{8,12},{9,13},{10,... | collective-permute-start | bytes 98312 | tf_op jit(solution)/shard_map/ppermute | solution.py:29
  145.7 104.6 %all-to-all-start.1 = ((bf16[32,1,64,128]{3,2,1,0:T(8,128)(2,1)}), bf16[32,1,64,128]{3,2,1,0:T(8,128)(2,1)}, u32[]{:S(2)}, u32[]{:S(2)}) async-start(bf16[32,1,64,128]{3,2,1,0:T(8,128)(2,1)} %copy.135), calls=%async_computation.1 | async-start | bytes 1048576 | tf_op jit(solution)/shard_map/all_to_all | solution.py:81
  151.0 97.7 %all-reduce.6.cloned.1.call-start = ((), (), s32[]{:S(2)}) async-start(), calls=%async_computation.2 | async-start | bytes 393216 | tf_op jit(solution)/shard_map/psum | solution.py:170
  (23 other events, 278.4 us)
Sparse Core Ops, SparseCore 0:
  157.7 90.9 all-reduce.5
